TPU v7x, 256 devices: a whole 4x4x8 slice. The times are simulated.
256 devices in a mesh: grp: 2 (over core), fsdp: 16 (over y, z_lo), tp: 8 (over x, z_hi).
Axes of the slice: x: 4, y: 4, z: 8 (z_hi: 2, z_lo: 4; z = z_hi * 4 + z_lo), core: 2. Of those that a mesh axis runs over, the one named last changes fastest.
Arguments:
- frames: bfloat16 [2, 4096, 8192], P('grp', 'fsdp'), may hold values from -6 to 6
- rewards: bfloat16 [4096], P('fsdp'), may hold values from -5 to 5
- actions: int32 [2, 4096], P('grp', 'fsdp'), may hold values from 0 to 17
- fractions: int32 [2, 4096, 32], P('grp', 'fsdp'), may hold values from 0 to 63
- episode_shard: int32 [4096, 1], P('fsdp'), may hold values from 0 to 15, as said below
- table: float32 [64], replicated, may hold values from 0.02 to 0.98
- norm_gain: float32 [8192], replicated, may hold values from 0.1 to 1.9
- torso_weight: bfloat16 [8192, 4096], P(('grp', 'fsdp'), 'tp'), may hold values from -0.0625 to 0.0625
- embed_weight: bfloat16 [64, 4096], P(None, 'tp'), may hold values from -0.75 to 0.75
- value_weight: bfloat16 [18, 4096], P(None, 'tp'), may hold values from -0.59765625 to 0.59765625
Outputs:
- torso_grad: float32 [8192, 4096], P(('grp', 'fsdp'), 'tp')
- refreshed_weight: bfloat16 [8192, 4096], P(('grp', 'fsdp', 'tp'))
Inputs may be any that keep to these rules, and one draw needn't show every extreme that they name: `episode_shard`: of the rows of one index of fsdp, at most 24 belong to one learner shard, and in every such block some learner shard gets exactly 24; every learner shard gets at least one row from every block.
All inputs are finite; a program needn't handle non-finite values.
Results may differ from a plain program's by a relative error of at most 0.0075.
Values may be sent and summed in bfloat16 or wider, within the bound.
No kernel may reach another device: no remote copies, remote signals or barrier semaphores. Data moves between devices by JAX's collectives and lax.ppermute only.
A program may use at most 64 MiB of HBM per device.

v0:
```python
import jax
import jax.numpy as jnp
from jax import lax
from jax.sharding import PartitionSpec as P

ACTIONS = 18
COSINES = 64
FRACS = 64
Z = 4
Y = 4
SWAP = [(0, 1), (1, 0)]


def z_from(step):
    return [(f, f // Z * Z + (f % Z - step) % Z) for f in range(Y * Z)]


def y_from(step):
    return [(f, (f - step * Z) % (Y * Z)) for f in range(Y * Z)]


def roll_from(array, start, axis):
    size = array.shape[axis]
    return lax.dynamic_slice_in_dim(jnp.concatenate([array, array], axis), start, size, axis)


def shards(
    frames,
    rewards,
    actions,
    fractions,
    episode_shard,
    table,
    norm_gain,
    torso_weight,
    embed_weight,
    value_weight,
):
    group = lax.axis_index("grp")
    place = lax.axis_index("fsdp")
    shard_total = lax.axis_size("fsdp")
    whole = lax.all_gather(torso_weight, ("grp", "fsdp"), axis=0, tiled=True)
    rows_block = frames.shape[1]
    width = frames.shape[2]
    half = rows_block // 2
    own_rows = group * half
    other_rows = (1 - group) * half

    def swap(array):
        kept = lax.dynamic_slice_in_dim(array, own_rows, half, 0)
        sent = lax.dynamic_slice_in_dim(array, other_rows, half, 0)
        got = lax.ppermute(sent, "grp", SWAP)
        return (jnp.where(group == 0, kept, got), jnp.where(group == 0, got, kept))

    with jax.named_scope("rows_swap"):
        target_rows, online_rows = swap(frames[0])
        ints = jnp.concatenate([fractions[0].T, actions[0][None, :]], 0)
        target_ints, online_ints = swap(ints.T)
        ints_all = jnp.concatenate([target_ints, online_ints], 0).T
        fraction_rows = ints_all[:-1]
        action_rows = ints_all[-1]

    def norm(rows):
        values = rows.astype(jnp.float32)
        mean_square = jnp.mean(values * values, axis=-1, keepdims=True)
        return (values * lax.rsqrt(mean_square + 1e-05) * norm_gain).astype(jnp.bfloat16)

    normed_target = norm(target_rows)
    normed_online = norm(online_rows)
    normed = jnp.concatenate([normed_target, normed_online], 0)
    with jax.named_scope("columns_exchange"):
        block = width // (2 * shard_total)
        own_cols = lax.dynamic_slice_in_dim(normed_online, group * (width // 2), width // 2, 1)
        other_cols = lax.dynamic_slice_in_dim(
            normed_online, (1 - group) * (width // 2), width // 2, 1
        )
        pieces = jnp.stack(
            [
                own_cols.reshape(half, shard_total, block),
                other_cols.reshape(half, shard_total, block),
            ],
            2,
        )
        pieces = jnp.transpose(pieces, (1, 0, 2, 3)).reshape(shard_total, half, 2 * block)
        columns = lax.all_to_all(pieces, "fsdp", 0, 0, tiled=True)
        columns = columns.reshape(Y, Z, half, 2 * block)
        columns = roll_from(roll_from(columns, place // Z, 0), place % Z, 1)
    with jax.named_scope("counts"):
        lanes = jnp.arange(shard_total, dtype=jnp.int32)
        onehot = episode_shard[:, :1] == lanes[None, :]
        local_counts = jnp.sum(onehot.astype(jnp.float32), axis=0)
        counts = jnp.sum(
            lax.all_to_all(
                jnp.broadcast_to(local_counts[None, :], (shard_total, shard_total)),
                "fsdp",
                0,
                0,
                tiled=True,
            ),
            axis=0,
        )
        inverse = float(rows_block) / counts
        row_weight = jnp.sum(jnp.where(onehot, inverse[None, :], 0.0), axis=1)
        row_weight = lax.dynamic_slice_in_dim(row_weight, own_rows, half, 0)
    choose_mask = (action_rows[:, None] == jnp.arange(ACTIONS, dtype=jnp.int32)[None, :]).astype(
        jnp.bfloat16
    )
    picked = jnp.dot(choose_mask, value_weight, preferred_element_type=jnp.float32)
    cosine = jnp.cos(
        jnp.pi * jnp.arange(COSINES, dtype=jnp.float32)[None, :] * table[:, None]
    ).astype(jnp.bfloat16)
    embedding = jax.nn.relu(
        jnp.dot(cosine, embed_weight, preferred_element_type=jnp.float32)
    ).astype(jnp.bfloat16)
    ids = jnp.arange(FRACS, dtype=jnp.int32)
    online_fractions = fraction_rows[:, half:]
    online_select = online_fractions[:, None, :] == ids[None, :, None]
    levels = jnp.sum(jnp.where(online_select, table[None, :, None], 0.0), axis=1)
    reward_rows = lax.dynamic_slice_in_dim(rewards, own_rows, half, 0).astype(jnp.float32)
    preact = jnp.dot(normed, whole, preferred_element_type=jnp.float32)
    weighted = (jax.nn.silu(preact) * picked).astype(jnp.bfloat16)
    table_values = lax.dot_general(
        embedding, weighted, (((1,), (1,)), ((), ())), preferred_element_type=jnp.float32
    )
    partial_quant = jnp.sum(
        jnp.where(fraction_rows[:, None, :] == ids[None, :, None], table_values[None, :, :], 0.0),
        axis=1,
    )
    with jax.named_scope("quant_sum"):
        tp_total = lax.axis_size("tp")
        quant = jnp.sum(
            lax.all_to_all(
                jnp.broadcast_to(partial_quant[None], (tp_total,) + partial_quant.shape),
                "tp",
                0,
                0,
                tiled=True,
            ),
            axis=0,
        )
    target_quant = quant[:, :half]
    online_quant = quant[:, half:]
    target_value = reward_rows[None, :] + 0.99 * target_quant
    errors = target_value[None, :, :] - online_quant[:, None, :]
    weight = jnp.abs(levels[:, None, :] - (errors < 0).astype(jnp.float32))
    grad_quant = -row_weight[None, :] * jnp.sum(weight * jnp.clip(errors, -1.0, 1.0), axis=1)
    grad_table = jnp.sum(jnp.where(online_select, grad_quant[:, None, :], 0.0), axis=0)
    grad_feature = lax.dot_general(
        grad_table,
        embedding.astype(jnp.float32),
        (((0,), (0,)), ((), ())),
        precision=lax.Precision.HIGHEST,
    )
    online_preact = preact[half:]
    gate_value = jax.nn.sigmoid(online_preact)
    grad_preact = (
        grad_feature * picked[half:] * gate_value * (1.0 + online_preact * (1.0 - gate_value))
    ).astype(jnp.bfloat16)
    with jax.named_scope("grad_gather"):
        quad = jnp.stack(
            [grad_preact] + [lax.ppermute(grad_preact, "fsdp", z_from(k)) for k in range(1, Z)]
        )
        below = lax.ppermute(quad, "fsdp", y_from(1))
        above = lax.ppermute(quad, "fsdp", y_from(3))
        far_low = lax.ppermute(above[: Z // 2], "fsdp", y_from(3))
        far_high = lax.ppermute(below[Z // 2 :], "fsdp", y_from(1))

    def product(cols, grads):
        return lax.dot_general(
            cols.reshape(-1, cols.shape[-1]),
            grads.reshape(-1, grads.shape[-1]),
            (((0,), (0,)), ((), ())),
            preferred_element_type=jnp.float32,
        )

    part = (
        product(columns[0], quad)
        + product(columns[1], below)
        + product(columns[3], above)
        + product(columns[2, : Z // 2], far_low)
        + product(columns[2, Z // 2 :], far_high)
    )
    torso_grad = part[:block] + lax.ppermute(part[block:], "grp", SWAP)
    updated = (torso_weight.astype(jnp.float32) - 0.01 * torso_grad).astype(jnp.bfloat16)
    refreshed_weight = lax.all_to_all(updated, "tp", split_axis=0, concat_axis=1, tiled=True)
    return (torso_grad, refreshed_weight)


def solution(mesh):
    placed = (
        P("grp", "fsdp", None),
        P("fsdp"),
        P("grp", "fsdp"),
        P("grp", "fsdp", None),
        P("fsdp", None),
        P(),
        P(),
        P(("grp", "fsdp"), "tp"),
        P(None, "tp"),
        P(None, "tp"),
    )
    return jax.shard_map(
        shards,
        mesh=mesh,
        in_specs=placed,
        out_specs=(P(("grp", "fsdp"), "tp"), P(("grp", "fsdp", "tp"), None)),
        check_vma=False,
    )
```

profile of v0, /device:TPU:1, one launch (start us, length us, event | category | flops | bytes accessed | tf_op | source)
XLA Modules:
  0.0 217.1 jit_solution(5258170492067754753)
XLA Ops:
  7.9 3.1 %dynamic-slice_bitcast_fusion = bf16[128,8192]{1,0:T(8,128)(2,1)} fusion(bf16[1,256,8192]{2,1,0:T(8,128)(2,1)} %param.10, s32[]{:T(128)S(6)} %select_n.74), kind=kLoop, calls=%fused_computation.25 | loop fusion | bytes 4194308 | tf_op jit(solution)/shard_map/rows_swap/dynamic_slice | solution.py:51
  11.1 3.2 %collective-permute-start = (bf16[128,8192]{1,0:T(8,128)(2,1)}, bf16[128,8192]{1,0:T(8,128)(2,1)S(1)}, u32[]{:S(2)}, u32[]{:S(2)}) collective-permute-start(bf16[128,8192]{1,0:T(8,128)(2,1)} %dynamic-slice_bitcast_fusion), channel_id=1, source_target_pairs={{0,128},{128,0},{1,129},{129,1},{2,130},{130,2},{3,131},{131,3},{4... | collective-permute-start | bytes 6291464 | tf_op jit(solution)/shard_map/rows_swap/ppermute | solution.py:52
  15.1 6.6 %all-to-all-start.1 = ((f32[16,1,16]{2,1,0:T(1,128)}), f32[16,1,16]{2,1,0:T(1,128)S(1)}, u32[]{:S(2)}, u32[]{:S(2)}) async-start(f32[16,1,16]{2,1,0:T(1,128)} %broadcast_in_dim.46), calls=%async_computation.1 | async-start | bytes 16384 | tf_op jit(solution)/shard_map/counts/all_to_all | solution.py:93
  21.7 3.9 %fusion.3 = (f32[128]{0:T(128)S(1)}, f32[128]{0:T(128)S(1)}) fusion(bf16[128,8192]{1,0:T(8,128)(2,1)S(1)} %collective-permute-done, bf16[1,256,8192]{2,1,0:T(8,128)(2,1)} %param.10, s32[]{:T(128)S(6)} %select_n.75, pred[]{:T(512)S(6)} %eq.32), kind=kLoop, calls=%fused_computation.7 | loop fusion | flops 8388352 | bytes 4195333 | tf_op jit(solution)/shard_map/reduce_sum | solution.py:65
  25.7 4.4 %fusion.5 = (bf16[128,8192]{1,0:T(8,128)(2,1)}, bf16[128,8192]{1,0:T(8,128)(2,1)S(1)}) fusion(f32[128]{0:T(128)S(1)} %get-tuple-element.19, f32[8192]{0:T(1024)S(1)} %copy-done.5, bf16[128,8192]{1,0:T(8,128)(2,1)} %copy-done.2, bf16[1,256,8192]{2,1,0:T(8,128)(2,1)S(1)} %copy-done.1, s32[]{:T(128)S(6)} %select_n.75, pred[]{:T(512)S(6)} %eq.32, ...), kind=kLoop, calls=%fused_computation.9 | loop fusion | flops 10485760 | bytes 8422405 | tf_op jit(solution)/shard_map/convert_element_type | solution.py:66
  30.1 1.2 constant_dynamic-slice_fusion.1
  31.3 2.3 %copy.29 = bf16[128,4096]{0,1:T(8,128)(2,1)} copy(bf16[128,4096]{1,0:T(8,128)(2,1)} %get-tuple-element.13) | data formatting | bytes 2097152 | tf_op jit(solution)/shard_map/columns_exchange/dynamic_slice | solution.py:73
  33.6 1.3 copy.30
  34.9 1.8 maximum_bitcast_fusion
  36.7 1.5 copy.31
  38.2 7.1 %all-to-all-start = ((bf16[16,128,512]{1,2,0:T(8,128)(2,1)}), bf16[16,128,512]{1,2,0:T(8,128)(2,1)}, u32[]{:S(2)}, u32[]{:S(2)}) async-start(bf16[16,128,512]{1,2,0:T(8,128)(2,1)} %bitcast.69), calls=%async_computation | async-start | bytes 4194304 | tf_op jit(solution)/shard_map/columns_exchange/all_to_all | solution.py:85
  45.3 0.9 collective-permute-start.1
  47.4 75.1 %all-gather.2.cloned.1.call-done = bf16[8192,512]{1,0:T(8,128)(2,1)} async-done(((bf16[256,512]{1,0:T(8,128)(2,1)}), bf16[8192,512]{1,0:T(8,128)(2,1)}) %all-gather.2.cloned.1.call-update) | async-done | bytes 8388624 | tf_op jit(solution)/shard_map/all_gather | solution.py:42
  122.5 6.3 %fusion.6 = f32[256,512]{1,0:T(8,128)S(1)} fusion(bf16[8192,512]{1,0:T(8,128)(2,1)} %all-gather.2.cloned.1.call-done, bf16[128,8192]{1,0:T(8,128)(2,1)S(1)} %get-tuple-element.7, bf16[128,8192]{1,0:T(8,128)(2,1)} %get-tuple-element.6), kind=kOutput, calls=%fused_computation.14 | convolution fusion | flops 2155872256 | bytes 13107200 | tf_op jit(solution)/shard_map/dot_general | solution.py:120
  128.8 0.8 copy-done.11
  131.0 7.4 %all-to-all-start.2 = ((f32[8,32,256]{2,1,0:T(8,128)}), f32[8,32,256]{2,1,0:T(8,128)S(1)}, u32[]{:S(2)}, u32[]{:S(2)}) async-start(f32[8,32,256]{2,1,0:T(8,128)} %broadcast_in_dim.53), calls=%async_computation.2 | async-start | bytes 524288 | tf_op jit(solution)/shard_map/quant_sum/all_to_all | solution.py:132
  138.8 2.8 %copy.32 = bf16[4,4,128,512]{3,2,1,0:T(8,128)(2,1)S(1)} copy(bf16[4,4,128,512]{2,3,1,0:T(8,128)(2,1)} %bitcast.6) | data formatting | bytes 4194304 | tf_op jit(solution)/shard_map/columns_exchange/reshape | solution.py:86
  141.6 7.7 %all-to-all-done.2 = f32[8,32,256]{2,1,0:T(8,128)S(1)} async-done(((f32[8,32,256]{2,1,0:T(8,128)}), f32[8,32,256]{2,1,0:T(8,128)S(1)}, u32[]{:S(2)}, u32[]{:S(2)}) %all-to-all-start.2) | async-done | bytes 262176 | tf_op jit(solution)/shard_map/quant_sum/all_to_all | solution.py:132
  149.7 1.3 fusion.16
  151.0 1.7 collective-permute-start.2
  152.7 2.3 %collective-permute-start.3 = (bf16[128,512]{1,0:T(8,128)(2,1)S(1)}, bf16[128,512]{1,0:T(8,128)(2,1)S(1)}, u32[]{:S(2)}, u32[]{:S(2)}) collective-permute-start(bf16[128,512]{1,0:T(8,128)(2,1)S(1)} %fusion.16), channel_id=1, source_target_pairs={{0,16},{8,24},{16,0},{24,8},{32,48},{40,56},{48,32},{56,40},{64,80... | collective-permute-start | bytes 393224 | tf_op jit(solution)/shard_map/grad_gather/ppermute | solution.py:161
  155.0 1.0 collective-permute-start.4
  156.8 4.7 %collective-permute-done.3 = bf16[128,512]{1,0:T(8,128)(2,1)S(1)} collective-permute-done((bf16[128,512]{1,0:T(8,128)(2,1)S(1)}, bf16[128,512]{1,0:T(8,128)(2,1)S(1)}, u32[]{:S(2)}, u32[]{:S(2)}) %collective-permute-start.3) | collective-permute-done | bytes 131104 | tf_op jit(solution)/shard_map/grad_gather/ppermute | solution.py:161
  161.4 1.5 collective-permute-done.4
  163.0 6.2 %collective-permute-start.5 = (bf16[4,128,512]{2,1,0:T(8,128)(2,1)S(1)}, bf16[4,128,512]{2,1,0:T(8,128)(2,1)S(1)}, u32[]{:S(2)}, u32[]{:S(2)}) collective-permute-start(bf16[4,128,512]{2,1,0:T(8,128)(2,1)S(1)} %pad_maximum_fusion), channel_id=1, source_target_pairs={{0,96},{8,104},{16,112},{24,120},{32,0},{40,8},{48,16},{56,24},{64... | collective-permute-start | bytes 1572872 | tf_op jit(solution)/shard_map/grad_gather/ppermute | solution.py:163
  170.5 11.6 %collective-permute-done.6 = bf16[4,128,512]{2,1,0:T(8,128)(2,1)S(1)} collective-permute-done((bf16[4,128,512]{2,1,0:T(8,128)(2,1)S(1)}, bf16[4,128,512]{2,1,0:T(8,128)(2,1)S(1)}, u32[]{:S(2)}, u32[]{:S(2)}) %collective-permute-start.6) | collective-permute-done | bytes 524320 | tf_op jit(solution)/shard_map/grad_gather/ppermute | solution.py:164
  182.3 2.7 %collective-permute-start.8 = (bf16[2,128,512]{2,1,0:T(8,128)(2,1)S(1)}, bf16[2,128,512]{2,1,0:T(8,128)(2,1)S(1)}, u32[]{:S(2)}, u32[]{:S(2)}) collective-permute-start(bf16[2,128,512]{2,1,0:T(8,128)(2,1)S(1)} %slice.78), channel_id=1, source_target_pairs={{0,96},{8,104},{16,112},{24,120},{32,0},{40,8},{48,16},{56,24},{64... | collective-permute-start | bytes 786440 | tf_op jit(solution)/shard_map/grad_gather/ppermute | solution.py:166
  186.0 2.7 %collective-permute-done.7 = bf16[2,128,512]{2,1,0:T(8,128)(2,1)S(1)} collective-permute-done((bf16[2,128,512]{2,1,0:T(8,128)(2,1)S(1)}, bf16[2,128,512]{2,1,0:T(8,128)(2,1)S(1)}, u32[]{:S(2)}, u32[]{:S(2)}) %collective-permute-start.7) | collective-permute-done | bytes 262176 | tf_op jit(solution)/shard_map/grad_gather/ppermute | solution.py:165
  189.9 3.8 %collective-permute-start.9 = (f32[256,512]{1,0:T(8,128)S(1)}, f32[256,512]{1,0:T(8,128)S(1)}, u32[]{:S(2)}, u32[]{:S(2)}) collective-permute-start(f32[256,512]{1,0:T(8,128)S(1)} %slice.80), channel_id=1, source_target_pairs={{0,128},{128,0},{1,129},{129,1},{2,130},{130,2},{3,131},{131,3},{4... | collective-permute-start | bytes 1572872 | tf_op jit(solution)/shard_map/ppermute | solution.py:183
  193.7 1.5 collective-permute-done.9
  195.2 0.9 subtract_convert_fusion
  196.2 13.3 %all_to_all.35 = bf16[8,32,512]{2,1,0:T(8,128)(2,1)S(1)} all-to-all(bf16[8,32,512]{2,1,0:T(8,128)(2,1)S(1)} %bitcast.81), channel_id=1, replica_groups=mesh['grp'=2,'fsdp'=16,'tp'=8] {'tp'}, dimensions={0} | all-to-all | bytes 524288 | tf_op jit(solution)/shard_map/all_to_all | solution.py:185
  (74 shorter events, 10.0 us)
Async XLA Ops:
  7.2 39.1 %copy-start = (bf16[64,512]{1,0:T(8,128)(2,1)S(1)}, bf16[64,512]{1,0:T(8,128)(2,1)}, u32[]{:S(2)}) copy-start(bf16[64,512]{1,0:T(8,128)(2,1)} %param.18) | copy-start | bytes 196612
  7.2 115.3 %all-gather.2.cloned.1.call-start = ((), (), s32[]{:S(2)}) async-start(), calls=%async_computation.4 | async-start | bytes 8650752 | tf_op jit(solution)/shard_map/all_gather | solution.py:42
  7.9 6.4 %copy-start.9 = (s32[256,1]{0,1:T(1,128)S(1)}, s32[256,1]{0,1:T(1,128)}, u32[]{:S(2)}) copy-start(s32[256,1]{0,1:T(1,128)} %param.14) | copy-start | bytes 3076
  7.9 17.7 %copy-start.5 = (f32[8192]{0:T(1024)S(1)}, f32[8192]{0:T(1024)}, u32[]{:S(2)}) copy-start(f32[8192]{0:T(1024)} %param.16) | copy-start | bytes 98308
  11.1 10.6 %collective-permute-start = (bf16[128,8192]{1,0:T(8,128)(2,1)}, bf16[128,8192]{1,0:T(8,128)(2,1)S(1)}, u32[]{:S(2)}, u32[]{:S(2)}) collective-permute-start(bf16[128,8192]{1,0:T(8,128)(2,1)} %dynamic-slice_bitcast_fusion), channel_id=1, source_target_pairs={{0,128},{128,0},{1,129},{129,1},{2,130},{130,2},{3,131},{131,3},{4... | collective-permute-start | bytes 6291464 | tf_op jit(solution)/shard_map/rows_swap/ppermute | solution.py:52
  15.1 23.1 %all-to-all-start.1 = ((f32[16,1,16]{2,1,0:T(1,128)}), f32[16,1,16]{2,1,0:T(1,128)S(1)}, u32[]{:S(2)}, u32[]{:S(2)}) async-start(f32[16,1,16]{2,1,0:T(1,128)} %broadcast_in_dim.46), calls=%async_computation.1 | async-start | bytes 16384 | tf_op jit(solution)/shard_map/counts/all_to_all | solution.py:93
  21.7 4.0 %copy-start.1 = (bf16[1,256,8192]{2,1,0:T(8,128)(2,1)S(1)}, bf16[1,256,8192]{2,1,0:T(8,128)(2,1)}, u32[]{:S(2)}) copy-start(bf16[1,256,8192]{2,1,0:T(8,128)(2,1)} %param.10) | copy-start | bytes 12582916
  21.7 3.9 %copy-start.2 = (bf16[128,8192]{1,0:T(8,128)(2,1)}, bf16[128,8192]{1,0:T(8,128)(2,1)S(1)}, u32[]{:S(2)}) copy-start(bf16[128,8192]{1,0:T(8,128)(2,1)S(1)} %collective-permute-done) | copy-start | bytes 6291460
  38.1 7.1 %copy-start.4 = (s32[1,256,32]{1,2,0:T(8,128)S(1)}, s32[1,256,32]{1,2,0:T(8,128)}, u32[]{:S(2)}) copy-start(s32[1,256,32]{1,2,0:T(8,128)} %param.13) | copy-start | bytes 98308
  38.1 7.2 %copy-start.7 = (s32[1,256]{1,0:T(1,128)S(1)}, s32[1,256]{1,0:T(1,128)}, u32[]{:S(2)}) copy-start(s32[1,256]{1,0:T(1,128)} %param.12) | copy-start | bytes 3076
  38.1 8.1 %copy-start.8 = (f32[64]{0:T(128)S(1)}, f32[64]{0:T(128)}, u32[]{:S(2)}) copy-start(f32[64]{0:T(128)} %param.15) | copy-start | bytes 772
  38.1 8.4 %copy-start.10 = (bf16[256]{0:T(256)(128)(2,1)S(1)}, bf16[256]{0:T(256)(128)(2,1)}, u32[]{:S(2)}) copy-start(bf16[256]{0:T(256)(128)(2,1)} %param.11) | copy-start | bytes 1540
  38.2 8.9 %copy-start.6 = (bf16[18,512]{1,0:T(8,128)(2,1)S(1)}, bf16[18,512]{1,0:T(8,128)(2,1)}, u32[]{:S(2)}) copy-start(bf16[18,512]{1,0:T(8,128)(2,1)} %param.19) | copy-start | bytes 55300
  38.2 92.1 %all-to-all-start = ((bf16[16,128,512]{1,2,0:T(8,128)(2,1)}), bf16[16,128,512]{1,2,0:T(8,128)(2,1)}, u32[]{:S(2)}, u32[]{:S(2)}) async-start(bf16[16,128,512]{1,2,0:T(8,128)(2,1)} %bitcast.69), calls=%async_computation | async-start | bytes 4194304 | tf_op jit(solution)/shard_map/columns_exchange/all_to_all | solution.py:85
  45.3 1.7 collective-permute-start.1
  128.8 0.8 copy-start.11
  131.0 18.3 %all-to-all-start.2 = ((f32[8,32,256]{2,1,0:T(8,128)}), f32[8,32,256]{2,1,0:T(8,128)S(1)}, u32[]{:S(2)}, u32[]{:S(2)}) async-start(f32[8,32,256]{2,1,0:T(8,128)} %broadcast_in_dim.53), calls=%async_computation.2 | async-start | bytes 524288 | tf_op jit(solution)/shard_map/quant_sum/all_to_all | solution.py:132
  151.0 5.8 %collective-permute-start.2 = (bf16[128,512]{1,0:T(8,128)(2,1)S(1)}, bf16[128,512]{1,0:T(8,128)(2,1)S(1)}, u32[]{:S(2)}, u32[]{:S(2)}) collective-permute-start(bf16[128,512]{1,0:T(8,128)(2,1)S(1)} %fusion.16), channel_id=1, source_target_pairs={{0,24},{8,0},{16,8},{24,16},{32,56},{40,32},{48,40},{56,48},{64,88... | collective-permute-start | bytes 393224 | tf_op jit(solution)/shard_map/grad_gather/ppermute | solution.py:161
  152.7 8.8 %collective-permute-start.3 = (bf16[128,512]{1,0:T(8,128)(2,1)S(1)}, bf16[128,512]{1,0:T(8,128)(2,1)S(1)}, u32[]{:S(2)}, u32[]{:S(2)}) collective-permute-start(bf16[128,512]{1,0:T(8,128)(2,1)S(1)} %fusion.16), channel_id=1, source_target_pairs={{0,16},{8,24},{16,0},{24,8},{32,48},{40,56},{48,32},{56,40},{64,80... | collective-permute-start | bytes 393224 | tf_op jit(solution)/shard_map/grad_gather/ppermute | solution.py:161
  155.0 7.9 %collective-permute-start.4 = (bf16[128,512]{1,0:T(8,128)(2,1)S(1)}, bf16[128,512]{1,0:T(8,128)(2,1)S(1)}, u32[]{:S(2)}, u32[]{:S(2)}) collective-permute-start(bf16[128,512]{1,0:T(8,128)(2,1)S(1)} %fusion.16), channel_id=1, source_target_pairs={{0,8},{8,16},{16,24},{24,0},{32,40},{40,48},{48,56},{56,32},{64,72... | collective-permute-start | bytes 393224 | tf_op jit(solution)/shard_map/grad_gather/ppermute | solution.py:161
  163.0 19.3 %collective-permute-start.5 = (bf16[4,128,512]{2,1,0:T(8,128)(2,1)S(1)}, bf16[4,128,512]{2,1,0:T(8,128)(2,1)S(1)}, u32[]{:S(2)}, u32[]{:S(2)}) collective-permute-start(bf16[4,128,512]{2,1,0:T(8,128)(2,1)S(1)} %pad_maximum_fusion), channel_id=1, source_target_pairs={{0,96},{8,104},{16,112},{24,120},{32,0},{40,8},{48,16},{56,24},{64... | collective-permute-start | bytes 1572872 | tf_op jit(solution)/shard_map/grad_gather/ppermute | solution.py:163
  169.2 13.0 %collective-permute-start.6 = (bf16[4,128,512]{2,1,0:T(8,128)(2,1)S(1)}, bf16[4,128,512]{2,1,0:T(8,128)(2,1)S(1)}, u32[]{:S(2)}, u32[]{:S(2)}) collective-permute-start(bf16[4,128,512]{2,1,0:T(8,128)(2,1)S(1)} %pad_maximum_fusion), channel_id=1, source_target_pairs={{0,32},{8,40},{16,48},{24,56},{32,64},{40,72},{48,80},{56,88},{64,... | collective-permute-start | bytes 1572872 | tf_op jit(solution)/shard_map/grad_gather/ppermute | solution.py:164
  182.2 6.5 %collective-permute-start.7 = (bf16[2,128,512]{2,1,0:T(8,128)(2,1)S(1)}, bf16[2,128,512]{2,1,0:T(8,128)(2,1)S(1)}, u32[]{:S(2)}, u32[]{:S(2)}) collective-permute-start(bf16[2,128,512]{2,1,0:T(8,128)(2,1)S(1)} %slice.76), channel_id=1, source_target_pairs={{0,32},{8,40},{16,48},{24,56},{32,64},{40,72},{48,80},{56,88},{64,... | collective-permute-start | bytes 786440 | tf_op jit(solution)/shard_map/grad_gather/ppermute | solution.py:165
  182.3 6.7 %collective-permute-start.8 = (bf16[2,128,512]{2,1,0:T(8,128)(2,1)S(1)}, bf16[2,128,512]{2,1,0:T(8,128)(2,1)S(1)}, u32[]{:S(2)}, u32[]{:S(2)}) collective-permute-start(bf16[2,128,512]{2,1,0:T(8,128)(2,1)S(1)} %slice.78), channel_id=1, source_target_pairs={{0,96},{8,104},{16,112},{24,120},{32,0},{40,8},{48,16},{56,24},{64... | collective-permute-start | bytes 786440 | tf_op jit(solution)/shard_map/grad_gather/ppermute | solution.py:166
  189.4 5.9 %copy-start.3 = (bf16[256,512]{1,0:T(8,128)(2,1)S(1)}, bf16[256,512]{1,0:T(8,128)(2,1)}, u32[]{:S(2)}) copy-start(bf16[256,512]{1,0:T(8,128)(2,1)} %param.17) | copy-start | bytes 786436
  189.9 5.3 %collective-permute-start.9 = (f32[256,512]{1,0:T(8,128)S(1)}, f32[256,512]{1,0:T(8,128)S(1)}, u32[]{:S(2)}, u32[]{:S(2)}) collective-permute-start(f32[256,512]{1,0:T(8,128)S(1)} %slice.80), channel_id=1, source_target_pairs={{0,128},{128,0},{1,129},{129,1},{2,130},{130,2},{3,131},{131,3},{4... | collective-permute-start | bytes 1572872 | tf_op jit(solution)/shard_map/ppermute | solution.py:183
Sparse Core Ops, SparseCore 0:
  9.9 112.5 all-gather.1
where the time goes:
time: 218 us; the launch traced here: 217 us
  waiting for transfers between devices  106 us (49%)
  starting transfers between devices  43.5 us (20%)
  local copies, waits for them, and re-layouts  15.3 us (7%)
  between operations  14.4 us (7%)
  other arithmetic  14 us (6%)
  blocking collectives  13.3 us (6%)
  matrix products  10.6 us (5%)
    all_gather x1, waiting for transfers between devices, shards(): whole = lax.all_gather(torso_weight, ('grp', 'fsdp'), axis=0, tiled=True)  75.1 us
    all_to_all x1, blocking collectives, shards(): lax.all_to_all(updated, 'tp', split_axis=0, concat_axis=1, tiled=True)  13.3 us
    ppermute x1, waiting for transfers between devices, shards(): above = lax.ppermute(quad, 'fsdp', y_from(3))  11.6 us
    all_to_all x1, waiting for transfers between devices, shards(): lax.all_to_all(jnp.broadcast_to(partial_quant[None], (tp_total,) + partia...  7.69 us
    all_to_all x1, starting transfers between devices, shards(): lax.all_to_all(jnp.broadcast_to(partial_quant[None], (tp_total,) + partia...  7.35 us
    all_to_all x1, starting transfers between devices, shards(): columns = lax.all_to_all(pieces, 'fsdp', 0, 0, tiled=True)  7.1 us
    all_to_all x1, starting transfers between devices, shards(): lax.all_to_all(jnp.broadcast_to(local_counts[None, :], (shard_total, shar...  6.62 us
    dot_general x1, matrix products, shards(): preact = jnp.dot(normed, whole, preferred_element_type=jnp.float32)  6.33 us
  transfers between devices with their start and end apart: 14, of which 8 were waited for; matrix products, arithmetic and copies ran while one was open for 16% of the time, Pallas kernels for 0%

commit v1 on v0

--- a/solution.py
+++ b/solution.py
@@ -39,7 +39,12 @@
     group = lax.axis_index("grp")
     place = lax.axis_index("fsdp")
     shard_total = lax.axis_size("fsdp")
-    whole = lax.all_gather(torso_weight, ("grp", "fsdp"), axis=0, tiled=True)
+    whole = jnp.concatenate(
+        lax.all_to_all(
+            jnp.stack([torso_weight] * lax.axis_size(("grp", "fsdp"))), ("grp", "fsdp"), 0, 0
+        ),
+        axis=0,
+    )
     rows_block = frames.shape[1]
     width = frames.shape[2]
     half = rows_block // 2

time: 218 us -> 347 us (1.59)
  waiting for transfers between devices: 106 us -> 232 us
  blocking collectives: 13.3 us -> 29 us
  between operations: 14.4 us -> 0.97 us
  starting transfers between devices: 43.5 us -> 35.7 us
  local copies, waits for them, and re-layouts: 15.3 us -> 19.7 us
    all_to_all x1, waiting for transfers between devices: 0.01 us -> 155 us  [shards(): lax.all_to_all(jnp.stack([torso_weight] * lax.axis_size(('grp', 'fsdp')))...]
    all_gather x1 -> x0, waiting for transfers between devices: 75.1 us -> none  [shards(): whole = lax.all_gather(torso_weight, ('grp', 'fsdp'), axis=0, tiled=True)]
    all_to_all x1, waiting for transfers between devices: 0.01 us -> 39.7 us  [shards(): columns = lax.all_to_all(pieces, 'fsdp', 0, 0, tiled=True)]
    all_to_all x0 -> x1, blocking collectives: none -> 15.7 us  [shards(): lax.all_to_all(jnp.broadcast_to(local_counts[None, :], (shard_total, shar...]
    another operation x0 -> x1, local copies, waits for them, and re-layouts: none -> 5.12 us  [shards(): jnp.stack([torso_weight] * lax.axis_size(('grp', 'fsdp')))]
    ppermute x1, starting transfers between devices: 6.18 us -> 2.01 us  [shards(): below = lax.ppermute(quad, 'fsdp', y_from(1))]
    ppermute x2, waiting for transfers between devices: 0.42 us -> 4.47 us  [swap(): got = lax.ppermute(sent, 'grp', SWAP)]
    ppermute x3, waiting for transfers between devices: 6.15 us -> 9.76 us  [shards(): lax.ppermute(grad_preact, 'fsdp', z_from(k))]
  transfers between devices with their start and end apart: 14 -> 13, of which waited for: 8 -> 10; matrix products, arithmetic and copies ran while one was open for 16% -> 10% of each run, Pallas kernels for 0% -> 0%
where the time goes in v1:
time: 347 us; the launch traced here: 343 us
  waiting for transfers between devices  232 us (67%)
  starting transfers between devices  35.7 us (10%)
  blocking collectives  29 us (8%)
  local copies, waits for them, and re-layouts  19.7 us (6%)
  other arithmetic  14.6 us (4%)
  matrix products  10.5 us (3%)
    all_to_all x1, waiting for transfers between devices, shards(): lax.all_to_all(jnp.stack([torso_weight] * lax.axis_size(('grp', 'fsdp')))...  155 us
    all_to_all x1, waiting for transfers between devices, shards(): columns = lax.all_to_all(pieces, 'fsdp', 0, 0, tiled=True)  39.7 us
    all_to_all x1, blocking collectives, shards(): lax.all_to_all(jnp.broadcast_to(local_counts[None, :], (shard_total, shar...  15.7 us
    all_to_all x1, blocking collectives, shards(): lax.all_to_all(updated, 'tp', split_axis=0, concat_axis=1, tiled=True)  13.3 us
    ppermute x1, waiting for transfers between devices, shards(): above = lax.ppermute(quad, 'fsdp', y_from(3))  11.9 us
    ppermute x3, waiting for transfers between devices, shards(): lax.ppermute(grad_preact, 'fsdp', z_from(k))  9.76 us
    all_to_all x1, starting transfers between devices, shards(): columns = lax.all_to_all(pieces, 'fsdp', 0, 0, tiled=True)  9.17 us
    all_to_all x1, starting transfers between devices, shards(): lax.all_to_all(jnp.broadcast_to(partial_quant[None], (tp_total,) + partia...  7.95 us
  transfers between devices with their start and end apart: 13, of which 10 were waited for; matrix products, arithmetic and copies ran while one was open for 10% of the time, Pallas kernels for 0%

profile of v1, /device:TPU:1, one launch (start us, length us, event | category | flops | bytes accessed | tf_op | source)
XLA Modules:
  0.0 342.6 jit_solution(107661394960980104)
XLA Ops:
  1.5 15.7 %all_to_all.40 = f32[16,1,16]{2,1,0:T(1,128)S(1)} all-to-all(f32[16,1,16]{2,1,0:T(1,128)S(1)} %broadcast_in_dim.46), channel_id=1, replica_groups=mesh['grp'=2,'fsdp'=16,'tp'=8] {'fsdp'}, dimensions={0} | all-to-all | bytes 2048 | tf_op jit(solution)/shard_map/counts/all_to_all | solution.py:98
  17.2 5.1 %stack.15 = bf16[32,256,512]{2,1,0:T(8,128)(2,1)} broadcast(bf16[256,512]{1,0:T(8,128)(2,1)} %param.17), dimensions={1,2} | broadcast | bytes 8650752 | tf_op jit(solution)/shard_map/stack | solution.py:44
  22.3 6.8 %all-to-all-start.2 = ((bf16[32,256,512]{2,1,0:T(8,128)(2,1)}), bf16[32,256,512]{2,1,0:T(8,128)(2,1)}, u32[]{:S(2)}, u32[]{:S(2)}) async-start(bf16[32,256,512]{2,1,0:T(8,128)(2,1)} %stack.15), calls=%async_computation.2 | async-start | bytes 16777216 | tf_op jit(solution)/shard_map/all_to_all | solution.py:43
  29.1 3.1 dynamic-slice_bitcast_fusion
  32.5 4.0 %collective-permute-done = bf16[128,8192]{1,0:T(8,128)(2,1)S(1)} collective-permute-done((bf16[128,8192]{1,0:T(8,128)(2,1)}, bf16[128,8192]{1,0:T(8,128)(2,1)S(1)}, u32[]{:S(2)}, u32[]{:S(2)}) %collective-permute-start) | collective-permute-done | bytes 2097184 | tf_op jit(solution)/shard_map/rows_swap/ppermute | solution.py:57
  36.6 3.9 %fusion.3 = (f32[128]{0:T(128)S(1)}, f32[128]{0:T(128)S(1)}) fusion(bf16[128,8192]{1,0:T(8,128)(2,1)S(1)} %collective-permute-done, bf16[1,256,8192]{2,1,0:T(8,128)(2,1)} %param.10, s32[]{:T(128)S(6)} %select_n.75, pred[]{:T(512)S(6)} %eq.32), kind=kLoop, calls=%fused_computation.7 | loop fusion | flops 8388352 | bytes 4195333 | tf_op jit(solution)/shard_map/reduce_sum | solution.py:70
  40.5 4.4 %fusion.5 = (bf16[128,8192]{1,0:T(8,128)(2,1)}, bf16[128,8192]{1,0:T(8,128)(2,1)S(1)}) fusion(f32[128]{0:T(128)S(1)} %get-tuple-element.19, f32[8192]{0:T(1024)S(1)} %copy-done.5, bf16[128,8192]{1,0:T(8,128)(2,1)} %copy-done.2, bf16[1,256,8192]{2,1,0:T(8,128)(2,1)S(1)} %copy-done.1, s32[]{:T(128)S(6)} %select_n.75, pred[]{:T(512)S(6)} %eq.32, ...), kind=kLoop, calls=%fused_computation.9 | loop fusion | flops 10485760 | bytes 8422405 | tf_op jit(solution)/shard_map/convert_element_type | solution.py:71
  44.9 1.2 constant_dynamic-slice_fusion.1
  46.1 2.3 copy.29
  48.3 1.3 copy.30
  49.6 1.7 maximum_bitcast_fusion
  51.4 1.4 copy.31
  52.8 155.1 %all-to-all-done.2 = bf16[32,256,512]{2,1,0:T(8,128)(2,1)} async-done(((bf16[32,256,512]{2,1,0:T(8,128)(2,1)}), bf16[32,256,512]{2,1,0:T(8,128)(2,1)}, u32[]{:S(2)}, u32[]{:S(2)}) %all-to-all-start.2) | async-done | bytes 8388640 | tf_op jit(solution)/shard_map/all_to_all | solution.py:43
  208.0 9.2 %all-to-all-start = ((bf16[16,128,512]{1,2,0:T(8,128)(2,1)}), bf16[16,128,512]{1,2,0:T(8,128)(2,1)}, u32[]{:S(2)}, u32[]{:S(2)}) async-start(bf16[16,128,512]{1,2,0:T(8,128)(2,1)} %bitcast.70), calls=%async_computation | async-start | bytes 4194304 | tf_op jit(solution)/shard_map/columns_exchange/all_to_all | solution.py:90
  217.2 1.2 collective-permute-start.1
  219.5 6.3 %fusion.6 = f32[256,512]{1,0:T(8,128)S(1)} fusion(bf16[8192,512]{1,0:T(8,128)(2,1)} %bitcast.15, bf16[128,8192]{1,0:T(8,128)(2,1)S(1)} %get-tuple-element.7, bf16[128,8192]{1,0:T(8,128)(2,1)} %get-tuple-element.6), kind=kOutput, calls=%fused_computation.14 | convolution fusion | flops 2155872256 | bytes 13107200 | tf_op jit(solution)/shard_map/dot_general | solution.py:125
  227.3 39.7 %all-to-all-done = bf16[16,128,512]{1,2,0:T(8,128)(2,1)} async-done(((bf16[16,128,512]{1,2,0:T(8,128)(2,1)}), bf16[16,128,512]{1,2,0:T(8,128)(2,1)}, u32[]{:S(2)}, u32[]{:S(2)}) %all-to-all-start) | async-done | bytes 2097184 | tf_op jit(solution)/shard_map/columns_exchange/all_to_all | solution.py:90
  267.7 7.9 %all-to-all-start.3 = ((f32[8,32,256]{2,1,0:T(8,128)}), f32[8,32,256]{2,1,0:T(8,128)S(1)}, u32[]{:S(2)}, u32[]{:S(2)}) async-start(f32[8,32,256]{2,1,0:T(8,128)} %broadcast_in_dim.53), calls=%async_computation.3 | async-start | bytes 524288 | tf_op jit(solution)/shard_map/quant_sum/all_to_all | solution.py:137
  276.1 2.8 copy.32
  278.9 6.8 %all-to-all-done.3 = f32[8,32,256]{2,1,0:T(8,128)S(1)} async-done(((f32[8,32,256]{2,1,0:T(8,128)}), f32[8,32,256]{2,1,0:T(8,128)S(1)}, u32[]{:S(2)}, u32[]{:S(2)}) %all-to-all-start.3) | async-done | bytes 262176 | tf_op jit(solution)/shard_map/quant_sum/all_to_all | solution.py:137
  286.1 1.3 fusion.16
  287.4 1.2 collective-permute-start.2
  289.7 1.6 collective-permute-done.2
  291.3 8.2 %collective-permute-done.3 = bf16[128,512]{1,0:T(8,128)(2,1)S(1)} collective-permute-done((bf16[128,512]{1,0:T(8,128)(2,1)S(1)}, bf16[128,512]{1,0:T(8,128)(2,1)S(1)}, u32[]{:S(2)}, u32[]{:S(2)}) %collective-permute-start.3) | collective-permute-done | bytes 131104 | tf_op jit(solution)/shard_map/grad_gather/ppermute | solution.py:166
  299.6 2.0 collective-permute-start.5
  302.5 11.9 %collective-permute-done.6 = bf16[4,128,512]{2,1,0:T(8,128)(2,1)S(1)} collective-permute-done((bf16[4,128,512]{2,1,0:T(8,128)(2,1)S(1)}, bf16[4,128,512]{2,1,0:T(8,128)(2,1)S(1)}, u32[]{:S(2)}, u32[]{:S(2)}) %collective-permute-start.6) | collective-permute-done | bytes 524320 | tf_op jit(solution)/shard_map/grad_gather/ppermute | solution.py:169
  314.5 2.7 collective-permute-start.8
  318.2 2.7 collective-permute-done.7
  322.1 4.0 %collective-permute-start.9 = (f32[256,512]{1,0:T(8,128)S(1)}, f32[256,512]{1,0:T(8,128)S(1)}, u32[]{:S(2)}, u32[]{:S(2)}) collective-permute-start(f32[256,512]{1,0:T(8,128)S(1)} %slice.80), channel_id=1, source_target_pairs={{0,128},{128,0},{1,129},{129,1},{2,130},{130,2},{3,131},{131,3},{4... | collective-permute-start | bytes 1572872 | tf_op jit(solution)/shard_map/ppermute | solution.py:188
  326.1 1.5 collective-permute-done.9
  327.6 0.9 subtract_convert_fusion
  328.6 13.3 %all_to_all.41 = bf16[8,32,512]{2,1,0:T(8,128)(2,1)S(1)} all-to-all(bf16[8,32,512]{2,1,0:T(8,128)(2,1)S(1)} %bitcast.82), channel_id=1, replica_groups=mesh['grp'=2,'fsdp'=16,'tp'=8] {'tp'}, dimensions={0} | all-to-all | bytes 524288 | tf_op jit(solution)/shard_map/all_to_all | solution.py:190
  (73 shorter events, 10.4 us)
Async XLA Ops:
  0.6 217.7 %copy-start = (bf16[64,512]{1,0:T(8,128)(2,1)S(1)}, bf16[64,512]{1,0:T(8,128)(2,1)}, u32[]{:S(2)}) copy-start(bf16[64,512]{1,0:T(8,128)(2,1)} %param.18) | copy-start | bytes 196612
  22.3 185.6 %all-to-all-start.2 = ((bf16[32,256,512]{2,1,0:T(8,128)(2,1)}), bf16[32,256,512]{2,1,0:T(8,128)(2,1)}, u32[]{:S(2)}, u32[]{:S(2)}) async-start(bf16[32,256,512]{2,1,0:T(8,128)(2,1)} %stack.15), calls=%async_computation.2 | async-start | bytes 16777216 | tf_op jit(solution)/shard_map/all_to_all | solution.py:43
  29.1 11.4 %copy-start.5 = (f32[8192]{0:T(1024)S(1)}, f32[8192]{0:T(1024)}, u32[]{:S(2)}) copy-start(f32[8192]{0:T(1024)} %param.16) | copy-start | bytes 98308
  32.2 4.4 %collective-permute-start = (bf16[128,8192]{1,0:T(8,128)(2,1)}, bf16[128,8192]{1,0:T(8,128)(2,1)S(1)}, u32[]{:S(2)}, u32[]{:S(2)}) collective-permute-start(bf16[128,8192]{1,0:T(8,128)(2,1)} %dynamic-slice_bitcast_fusion), channel_id=1, source_target_pairs={{0,128},{128,0},{1,129},{129,1},{2,130},{130,2},{3,131},{131,3},{4... | collective-permute-start | bytes 6291464 | tf_op jit(solution)/shard_map/rows_swap/ppermute | solution.py:57
  32.5 7.9 %copy-start.1 = (bf16[1,256,8192]{2,1,0:T(8,128)(2,1)S(1)}, bf16[1,256,8192]{2,1,0:T(8,128)(2,1)}, u32[]{:S(2)}) copy-start(bf16[1,256,8192]{2,1,0:T(8,128)(2,1)} %param.10) | copy-start | bytes 12582916
  36.6 3.9 %copy-start.2 = (bf16[128,8192]{1,0:T(8,128)(2,1)}, bf16[128,8192]{1,0:T(8,128)(2,1)S(1)}, u32[]{:S(2)}) copy-start(bf16[128,8192]{1,0:T(8,128)(2,1)S(1)} %collective-permute-done) | copy-start | bytes 6291460
  207.9 9.2 %copy-start.4 = (s32[1,256,32]{1,2,0:T(8,128)S(1)}, s32[1,256,32]{1,2,0:T(8,128)}, u32[]{:S(2)}) copy-start(s32[1,256,32]{1,2,0:T(8,128)} %param.13) | copy-start | bytes 98308
  207.9 9.2 %copy-start.7 = (s32[1,256]{1,0:T(1,128)S(1)}, s32[1,256]{1,0:T(1,128)}, u32[]{:S(2)}) copy-start(s32[1,256]{1,0:T(1,128)} %param.12) | copy-start | bytes 3076
  207.9 10.4 %copy-start.8 = (f32[64]{0:T(128)S(1)}, f32[64]{0:T(128)}, u32[]{:S(2)}) copy-start(f32[64]{0:T(128)} %param.15) | copy-start | bytes 772
  207.9 10.7 %copy-start.10 = (bf16[256]{0:T(256)(128)(2,1)S(1)}, bf16[256]{0:T(256)(128)(2,1)}, u32[]{:S(2)}) copy-start(bf16[256]{0:T(256)(128)(2,1)} %param.11) | copy-start | bytes 1540
  207.9 11.3 %copy-start.6 = (bf16[18,512]{1,0:T(8,128)(2,1)S(1)}, bf16[18,512]{1,0:T(8,128)(2,1)}, u32[]{:S(2)}) copy-start(bf16[18,512]{1,0:T(8,128)(2,1)} %param.19) | copy-start | bytes 55300
  208.0 59.0 %all-to-all-start = ((bf16[16,128,512]{1,2,0:T(8,128)(2,1)}), bf16[16,128,512]{1,2,0:T(8,128)(2,1)}, u32[]{:S(2)}, u32[]{:S(2)}) async-start(bf16[16,128,512]{1,2,0:T(8,128)(2,1)} %bitcast.70), calls=%async_computation | async-start | bytes 4194304 | tf_op jit(solution)/shard_map/columns_exchange/all_to_all | solution.py:90
  217.2 2.0 collective-permute-start.1
  225.8 0.8 copy-start.11
  226.6 49.0 %copy-start.9 = (s32[256,1]{0,1:T(1,128)S(1)}, s32[256,1]{0,1:T(1,128)}, u32[]{:S(2)}) copy-start(s32[256,1]{0,1:T(1,128)} %param.14) | copy-start | bytes 3076
  267.7 18.0 %all-to-all-start.3 = ((f32[8,32,256]{2,1,0:T(8,128)}), f32[8,32,256]{2,1,0:T(8,128)S(1)}, u32[]{:S(2)}, u32[]{:S(2)}) async-start(f32[8,32,256]{2,1,0:T(8,128)} %broadcast_in_dim.53), calls=%async_computation.3 | async-start | bytes 524288 | tf_op jit(solution)/shard_map/quant_sum/all_to_all | solution.py:137
  287.4 3.9 %collective-permute-start.2 = (bf16[128,512]{1,0:T(8,128)(2,1)S(1)}, bf16[128,512]{1,0:T(8,128)(2,1)S(1)}, u32[]{:S(2)}, u32[]{:S(2)}) collective-permute-start(bf16[128,512]{1,0:T(8,128)(2,1)S(1)} %fusion.16), channel_id=1, source_target_pairs={{0,24},{8,0},{16,8},{24,16},{32,56},{40,32},{48,40},{56,48},{64,88... | collective-permute-start | bytes 393224 | tf_op jit(solution)/shard_map/grad_gather/ppermute | solution.py:166
  288.6 10.9 %collective-permute-start.3 = (bf16[128,512]{1,0:T(8,128)(2,1)S(1)}, bf16[128,512]{1,0:T(8,128)(2,1)S(1)}, u32[]{:S(2)}, u32[]{:S(2)}) collective-permute-start(bf16[128,512]{1,0:T(8,128)(2,1)S(1)} %fusion.16), channel_id=1, source_target_pairs={{0,16},{8,24},{16,0},{24,8},{32,48},{40,56},{48,32},{56,40},{64,80... | collective-permute-start | bytes 393224 | tf_op jit(solution)/shard_map/grad_gather/ppermute | solution.py:166
  288.6 10.9 %collective-permute-start.4 = (bf16[128,512]{1,0:T(8,128)(2,1)S(1)}, bf16[128,512]{1,0:T(8,128)(2,1)S(1)}, u32[]{:S(2)}, u32[]{:S(2)}) collective-permute-start(bf16[128,512]{1,0:T(8,128)(2,1)S(1)} %fusion.16), channel_id=1, source_target_pairs={{0,8},{8,16},{16,24},{24,0},{32,40},{40,48},{48,56},{56,32},{64,72... | collective-permute-start | bytes 393224 | tf_op jit(solution)/shard_map/grad_gather/ppermute | solution.py:166
  299.6 14.9 %collective-permute-start.5 = (bf16[4,128,512]{2,1,0:T(8,128)(2,1)S(1)}, bf16[4,128,512]{2,1,0:T(8,128)(2,1)S(1)}, u32[]{:S(2)}, u32[]{:S(2)}) collective-permute-start(bf16[4,128,512]{2,1,0:T(8,128)(2,1)S(1)} %pad_maximum_fusion), channel_id=1, source_target_pairs={{0,96},{8,104},{16,112},{24,120},{32,0},{40,8},{48,16},{56,24},{64... | collective-permute-start | bytes 1572872 | tf_op jit(solution)/shard_map/grad_gather/ppermute | solution.py:168
  301.6 12.8 %collective-permute-start.6 = (bf16[4,128,512]{2,1,0:T(8,128)(2,1)S(1)}, bf16[4,128,512]{2,1,0:T(8,128)(2,1)S(1)}, u32[]{:S(2)}, u32[]{:S(2)}) collective-permute-start(bf16[4,128,512]{2,1,0:T(8,128)(2,1)S(1)} %pad_maximum_fusion), channel_id=1, source_target_pairs={{0,32},{8,40},{16,48},{24,56},{32,64},{40,72},{48,80},{56,88},{64,... | collective-permute-start | bytes 1572872 | tf_op jit(solution)/shard_map/grad_gather/ppermute | solution.py:169
  314.4 6.5 %collective-permute-start.7 = (bf16[2,128,512]{2,1,0:T(8,128)(2,1)S(1)}, bf16[2,128,512]{2,1,0:T(8,128)(2,1)S(1)}, u32[]{:S(2)}, u32[]{:S(2)}) collective-permute-start(bf16[2,128,512]{2,1,0:T(8,128)(2,1)S(1)} %slice.76), channel_id=1, source_target_pairs={{0,32},{8,40},{16,48},{24,56},{32,64},{40,72},{48,80},{56,88},{64,... | collective-permute-start | bytes 786440 | tf_op jit(solution)/shard_map/grad_gather/ppermute | solution.py:170
  314.5 6.7 %collective-permute-start.8 = (bf16[2,128,512]{2,1,0:T(8,128)(2,1)S(1)}, bf16[2,128,512]{2,1,0:T(8,128)(2,1)S(1)}, u32[]{:S(2)}, u32[]{:S(2)}) collective-permute-start(bf16[2,128,512]{2,1,0:T(8,128)(2,1)S(1)} %slice.78), channel_id=1, source_target_pairs={{0,96},{8,104},{16,112},{24,120},{32,0},{40,8},{48,16},{56,24},{64... | collective-permute-start | bytes 786440 | tf_op jit(solution)/shard_map/grad_gather/ppermute | solution.py:171
  321.6 6.1 %copy-start.3 = (bf16[256,512]{1,0:T(8,128)(2,1)S(1)}, bf16[256,512]{1,0:T(8,128)(2,1)}, u32[]{:S(2)}) copy-start(bf16[256,512]{1,0:T(8,128)(2,1)} %param.17) | copy-start | bytes 786436
  322.1 5.5 %collective-permute-start.9 = (f32[256,512]{1,0:T(8,128)S(1)}, f32[256,512]{1,0:T(8,128)S(1)}, u32[]{:S(2)}, u32[]{:S(2)}) collective-permute-start(f32[256,512]{1,0:T(8,128)S(1)} %slice.80), channel_id=1, source_target_pairs={{0,128},{128,0},{1,129},{129,1},{2,130},{130,2},{3,131},{131,3},{4... | collective-permute-start | bytes 1572872 | tf_op jit(solution)/shard_map/ppermute | solution.py:188
